TPU v7x, 256 devices: a whole 4x4x8 slice. The times are simulated.
256 devices in a mesh: dp: 8 (over x, y_hi), seq: 32 (over y_lo, z, core).
Axes of the slice: x: 4, y: 4 (y_hi: 2, y_lo: 2; y = y_hi * 2 + y_lo), z: 8, core: 2. Of those that a mesh axis runs over, the one named last changes fastest.
Arguments:
- inputs: bfloat16 [8, 16384, 1024], P('dp', 'seq'), may hold values from -6 to 6
- out_grad: bfloat16 [8, 16384, 1024], P('dp', 'seq'), may hold values from -6 to 6
- w_in: bfloat16 [1024, 3072], replicated, may hold values from -0.1875 to 0.1875
- taps: float32 [3, 3072], replicated, may hold values from -3 to 3
- filt: bfloat16 [64, 256, 1024], P(None, 'seq'), may hold values from -4 to 4
Outputs:
- mixed: bfloat16 [8, 16384, 1024], P('dp', 'seq')
- in_grad: bfloat16 [8, 16384, 1024], P('dp', 'seq')
- w_in_grad: float32 [1024, 3072], P('dp', 'seq')
- taps_grad: float32 [3, 3072], replicated
All inputs are finite; a program needn't handle non-finite values.
Results may differ from a plain program's by a relative error of at most 0.012.
Values may be sent and summed in bfloat16 or wider, within the bound.
A program may use at most 128 MiB of HBM per device.

v0:
```python
import math
import jax
import jax.numpy as jnp
from jax import lax
from jax.sharding import PartitionSpec as P

BLK = 256


def padded(cells, sides, width):
    for axis, dim in sides:
        count = lax.axis_size(axis)
        ends = count - 1
        head = lax.slice_in_dim(cells, 0, width, axis=dim)
        tail = lax.slice_in_dim(cells, cells.shape[dim] - width, cells.shape[dim], axis=dim)
        cells = jnp.concatenate(
            [
                lax.ppermute(tail, axis, [(i, (i + 1) % count) for i in range(ends)]),
                cells,
                lax.ppermute(head, axis, [((i + 1) % count, i) for i in range(ends)]),
            ],
            axis=dim,
        )
    return cells


def dct_table(count):
    rows = jnp.arange(count, dtype=jnp.float32)[:, None]
    cols = jnp.arange(count, dtype=jnp.float32)[None, :]
    first = jnp.where(rows == 0, jnp.float32(math.sqrt(0.5)), jnp.float32(1.0))
    table = (
        jnp.float32(math.sqrt(2.0 / count))
        * first
        * jnp.cos(jnp.float32(math.pi) * (cols + 0.5) * rows / count)
    )
    return table.astype(jnp.bfloat16)


def block_section(blocks, table_q):
    return jnp.einsum("rq,nbqd->nbrd", table_q, blocks, preferred_element_type=jnp.float32).astype(
        jnp.bfloat16
    )


def span_section(columns, filt, table_p):
    stack, span, narrow, width = columns.shape
    flat = columns.reshape(stack, span, narrow * width)
    second = jnp.einsum("ap,npk->nak", table_p, flat, preferred_element_type=jnp.float32)
    scaled = (filt.reshape(1, span, narrow * width).astype(jnp.float32) * second).astype(
        jnp.bfloat16
    )
    third = jnp.einsum("ap,nak->npk", table_p, scaled, preferred_element_type=jnp.float32).astype(
        jnp.bfloat16
    )
    return third.reshape(columns.shape)


def final_section(blocks, table_q):
    return jnp.einsum("rq,nbrd->nbqd", table_q, blocks, preferred_element_type=jnp.float32)


def shards(inputs, out_grad, w_in, taps, filt):
    tok = inputs.shape[1]
    width = inputs.shape[2]
    nseq = lax.axis_size("seq")
    ndata = lax.axis_size("dp")
    nblocks = tok // BLK
    table_q = dct_table(BLK)
    table_p = dct_table(filt.shape[0])
    factor = 1.0 / math.sqrt(ndata * nseq * tok)
    rows = inputs[0]
    z = jnp.dot(rows, w_in, preferred_element_type=jnp.float32).astype(jnp.bfloat16)
    zpad = padded(z, (("seq", 0),), 1)
    s = taps[0] * zpad[:-2] + taps[1] * zpad[1:-1] + taps[2] * zpad[2:]
    a_part = s[:, :width]
    g_part = s[:, width : 2 * width]
    v_part = s[:, 2 * width :]
    w = (a_part * v_part).astype(jnp.bfloat16)
    gradf = out_grad[0].astype(jnp.float32)
    e4 = (gradf * g_part).astype(jnp.bfloat16)
    columns = lax.all_to_all(
        block_section(w.reshape(1, nblocks, BLK, width), table_q),
        "seq",
        split_axis=2,
        concat_axis=1,
        tiled=True,
    )
    back = lax.all_to_all(
        span_section(columns, filt, table_p), "seq", split_axis=1, concat_axis=2, tiled=True
    )
    h4 = final_section(back, table_q).reshape(tok, width)
    grad_cols = lax.all_to_all(
        block_section(e4.reshape(1, nblocks, BLK, width), table_q),
        "seq",
        split_axis=2,
        concat_axis=1,
        tiled=True,
    )
    grad_back = lax.all_to_all(
        span_section(grad_cols, filt, table_p), "seq", split_axis=1, concat_axis=2, tiled=True
    )
    dw = final_section(grad_back, table_q).reshape(tok, width)
    mixed = (g_part * h4).astype(jnp.bfloat16)
    ds = jnp.concatenate([dw * v_part, gradf * h4, dw * a_part], axis=1).astype(jnp.bfloat16)
    dspad = padded(ds, (("seq", 0),), 1)
    du = (taps[0] * dspad[2:] + taps[1] * dspad[1:-1] + taps[2] * dspad[:-2]).astype(jnp.bfloat16)
    in_grad = jnp.dot(du, w_in.T, preferred_element_type=jnp.float32).astype(jnp.bfloat16)
    dsf = ds.astype(jnp.float32)
    zf = zpad.astype(jnp.float32)
    local_taps = jnp.stack([jnp.sum(dsf * zf[k : k + tok], axis=0) for k in range(3)])
    taps_grad = lax.psum(local_taps, ("dp", "seq")) * factor
    contract = (((0,), (0,)), ((), ()))
    partial_sum = lax.psum_scatter(
        lax.dot_general(rows, du, contract, preferred_element_type=jnp.float32),
        "dp",
        scatter_dimension=0,
        tiled=True,
    )
    w_grad = lax.psum_scatter(partial_sum, "seq", scatter_dimension=1, tiled=True) * factor
    return (mixed[None], in_grad[None], w_grad, taps_grad)


def solution(mesh):
    return jax.shard_map(
        shards,
        mesh=mesh,
        in_specs=(P("dp", "seq", None), P("dp", "seq", None), P(), P(), P(None, "seq", None)),
        out_specs=(P("dp", "seq", None), P("dp", "seq", None), P("dp", "seq"), P()),
        check_vma=False,
    )
```

profile of v0, /device:TPU:2, one launch (start us, length us, event | category | flops | bytes accessed | tf_op | source)
XLA Modules:
  0.0 500.8 jit_solution(6452901341456452620)
XLA Ops:
  7.2 1.2 copy-done
  8.4 6.4 %convolution_convert_fusion.2 = bf16[512,3072]{1,0:T(8,128)(2,1)S(1)} fusion(bf16[1024,3072]{1,0:T(8,128)(2,1)} %param.7, bf16[1,512,1024]{2,1,0:T(8,128)(2,1)S(1)} %copy-done), kind=kOutput, calls=%fused_computation.22 | convolution fusion | flops 3222798336 | bytes 10485760 | tf_op jit(solution)/shard_map/dot_general | solution.py:72
  14.9 2.0 collective-permute-start
  16.9 1.3 collective-permute-start.1
  18.2 3.4 collective-permute-done.1
  21.6 2.5 multiply_add_fusion
  24.2 2.7 copy-done.2
  26.8 0.3 fusion.12
  27.2 1.4 fusion.19
  28.6 2.1 copy.34
  30.7 11.8 %all-to-all-start.2 = ((bf16[1,2,256,1024]{3,1,0,2:T(2,128)(2,1)}), bf16[1,2,256,1024]{3,1,0,2:T(2,128)(2,1)S(1)}, u32[]{:S(2)}, u32[]{:S(2)}) async-start(bf16[1,2,256,1024]{3,1,0,2:T(2,128)(2,1)} %copy.34), calls=%async_computation.2 | async-start | bytes 2097152 | tf_op jit(solution)/shard_map/all_to_all | solution.py:92
  42.6 1.6 reshape.130
  44.2 26.7 %all-to-all-done.2 = bf16[1,2,256,1024]{3,1,0,2:T(2,128)(2,1)S(1)} async-done(((bf16[1,2,256,1024]{3,1,0,2:T(2,128)(2,1)}), bf16[1,2,256,1024]{3,1,0,2:T(2,128)(2,1)S(1)}, u32[]{:S(2)}, u32[]{:S(2)}) %all-to-all-start.2) | async-done | bytes 1048608 | tf_op jit(solution)/shard_map/all_to_all | solution.py:92
  70.9 0.3 copy.59
  71.1 0.1 copy.36
  71.2 1.6 copy.47
  72.8 3.8 convolution_convert_fusion
  76.7 2.0 copy.48
  78.6 0.1 bitcast_bitcast_fusion
  78.7 32.2 %all_to_all.60 = bf16[1,64,8,1024]{3,2,0,1:T(8,128)(2,1)S(1)} all-to-all(bf16[1,64,8,1024]{3,2,0,1:T(8,128)(2,1)S(1)} %bitcast_bitcast_fusion), channel_id=1, replica_groups=mesh['dp'=8,'seq'=32] {'seq'}, dimensions={1} | all-to-all | bytes 2097152 | tf_op jit(solution)/shard_map/all_to_all | solution.py:99
  111.0 1.3 fusion.20
  112.3 2.2 fusion.14
  114.5 2.4 fusion.18
  116.9 3.7 copy.27
  120.6 32.4 %all_to_all.61 = bf16[1,2,256,1024]{3,1,0,2:T(2,128)(2,1)S(1)} all-to-all(bf16[1,2,256,1024]{3,1,0,2:T(2,128)(2,1)} %copy.27), channel_id=1, replica_groups=mesh['dp'=8,'seq'=32] {'seq'}, dimensions={2} | all-to-all | bytes 2097152 | tf_op jit(solution)/shard_map/all_to_all | solution.py:81
  153.1 0.3 copy.60
  153.4 0.1 copy.29
  153.4 1.6 copy.45
  155.0 3.2 convolution_convert_fusion.1
  158.2 1.9 copy.46
  160.1 0.1 bitcast_bitcast_fusion.1
  160.2 32.4 %all_to_all.62 = bf16[1,64,8,1024]{3,2,0,1:T(8,128)(2,1)S(1)} all-to-all(bf16[1,64,8,1024]{3,2,0,1:T(8,128)(2,1)S(1)} %bitcast_bitcast_fusion.1), channel_id=1, replica_groups=mesh['dp'=8,'seq'=32] {'seq'}, dimensions={1} | all-to-all | bytes 2097152 | tf_op jit(solution)/shard_map/all_to_all | solution.py:88
  192.6 1.3 fusion.22
  193.9 3.2 fusion.13
  197.2 0.3 pad_maximum_fusion.8
  197.4 1.3 collective-permute-start.2
  198.7 3.0 collective-permute-start.3
  201.8 0.8 collective-permute-done.3
  202.6 12.4 %convolution_bitcast_fusion.2 = f32[1024,3072]{0,1:T(8,128)} fusion(bf16[1,512,1024]{2,1,0:T(8,128)(2,1)S(1)} %copy-done, bf16[1,3072]{1,0:T(2,128)(2,1)S(1)} %collective-permute-done.3, bf16[512,1024]{1,0:T(8,128)(2,1)S(1)} %copy-done.6, bf16[512,1024]{1,0:T(8,128)(2,1)S(1)} %get-tuple-element.14, bf16[512,1024]{1,0:T(8,128)(2,1)S(1)} %copy-done.5, ...), kind=kOutput, calls=%fused_computation.14 | convolution fusion | flops 3265265664 | bytes 16826368 | tf_op jit(solution)/shard_map/dot_general | solution.py:114
  215.0 0.3 reduce-scatter.5.cloned.1.call-start
  215.3 5.5 %maximum_convert_fusion = f32[514,3072]{1,0:T(8,128)} fusion(bf16[1,3072]{1,0:T(2,128)(2,1)S(1)} %collective-permute-done.1, bf16[512,3072]{1,0:T(8,128)(2,1)} %copy-done.4, bf16[1,3072]{1,0:T(2,128)(2,1)S(1)} %collective-permute-done), kind=kLoop, calls=%fused_computation.23 | loop fusion | flops 9474048 | bytes 9474048 | tf_op jit(solution)/shard_map/convert_element_type | solution.py:109
  220.7 152.5 %reduce-scatter.3.cloned.1.call-done = f32[128,3072]{0,1:T(8,128)} async-done(((f32[1024,3072]{0,1:T(8,128)}), f32[128,3072]{0,1:T(8,128)}) %reduce-scatter.3.cloned.1.call-update) | async-done | bytes 1572880 | tf_op jit(solution)/shard_map/reduce_scatter | solution.py:113
  373.3 9.3 %fusion.9 = (f32[3072]{0:T(1024)S(1)}, f32[3072]{0:T(1024)S(1)}, f32[3072]{0:T(1024)S(1)}) fusion(f32[514,3072]{1,0:T(8,128)} %maximum_convert_fusion, bf16[512,1024]{1,0:T(8,128)(2,1)S(1)} %copy-done.6, bf16[512,1024]{1,0:T(8,128)(2,1)S(1)} %copy-done.8, bf16[512,1024]{1,0:T(8,128)(2,1)S(1)} %copy-done.5), kind=kLoop, calls=%fused_computation.18 | loop fusion | flops 18865152 | bytes 22056960 | tf_op jit(solution)/shard_map/reduce_sum | solution.py:110
  382.7 75.7 %psum.7 = f32[3,3072]{1,0:T(4,128)S(1)} all-reduce(f32[3,3072]{1,0:T(4,128)S(1)} %pad_maximum_fusion.9), channel_id=1, replica_groups=mesh['dp'=8,'seq'=32] {'dp','seq'}, use_global_device_ids=true, to_apply=%region_5.6 | all-reduce | flops 9216 | bytes 73728 | tf_op jit(solution)/shard_map/psum | solution.py:111
  458.4 0.6 broadcast_multiply_fusion
  459.0 11.0 %fusion.17 = bf16[1,512,1024]{2,1,0:T(8,128)(2,1)} fusion(bf16[1024,3072]{1,0:T(8,128)(2,1)} %param.7, bf16[1,3072]{1,0:T(2,128)(2,1)S(1)} %collective-permute-done.3, bf16[512,1024]{1,0:T(8,128)(2,1)S(1)} %copy-done.6, bf16[512,1024]{1,0:T(8,128)(2,1)} %copy-done.7, bf16[512,1024]{1,0:T(8,128)(2,1)S(1)} %copy-done.5, ...), kind=kOutput, calls=%fused_computation.47 | convolution fusion | flops 3265789952 | bytes 10534912 | tf_op jit(solution)/shard_map/dot_general | solution.py:107
  470.0 22.5 %reduce-scatter.5.cloned.1.call-done = f32[128,96]{0,1:T(8,128)} async-done(((f32[128,3072]{0,1:T(8,128)}), f32[128,96]{0,1:T(8,128)}) %reduce-scatter.5.cloned.1.call-update) | async-done | bytes 49168 | tf_op jit(solution)/shard_map/reduce_scatter | solution.py:119
  492.5 1.4 broadcast_multiply_fusion.1
  (40 shorter events, 0.3 us)
Async XLA Ops:
  7.2 1.2 copy-start
  7.2 11.0 %copy-start.12 = (f32[3,3072]{1,0:T(4,128)S(1)}, f32[3,3072]{1,0:T(4,128)}, u32[]{:S(2)}) copy-start(f32[3,3072]{1,0:T(4,128)} %param.8) | copy-start | bytes 110596
  14.8 12.4 %copy-start.4 = (bf16[512,3072]{1,0:T(8,128)(2,1)}, bf16[512,3072]{1,0:T(8,128)(2,1)S(1)}, u32[]{:S(2)}) copy-start(bf16[512,3072]{1,0:T(8,128)(2,1)S(1)} %convolution_convert_fusion.2) | copy-start | bytes 9437188
  14.8 12.0 %copy-start.9 = (bf16[1,512,1024]{2,1,0:T(8,128)(2,1)S(1)}, bf16[1,512,1024]{2,1,0:T(8,128)(2,1)}, u32[]{:S(2)}) copy-start(bf16[1,512,1024]{2,1,0:T(8,128)(2,1)} %param.6) | copy-start | bytes 3145732
  14.9 3.4 collective-permute-start
  16.9 4.8 collective-permute-start.1
  24.2 2.7 copy-start.2
  26.8 15.7 %copy-start.11 = (bf16[64,8,1024]{2,1,0:T(8,128)(2,1)S(1)}, bf16[64,8,1024]{2,1,0:T(8,128)(2,1)}, u32[]{:S(2)}) copy-start(bf16[64,8,1024]{2,1,0:T(8,128)(2,1)} %param.9) | copy-start | bytes 3145732
  30.7 40.1 %all-to-all-start.2 = ((bf16[1,2,256,1024]{3,1,0,2:T(2,128)(2,1)}), bf16[1,2,256,1024]{3,1,0,2:T(2,128)(2,1)S(1)}, u32[]{:S(2)}, u32[]{:S(2)}) async-start(bf16[1,2,256,1024]{3,1,0,2:T(2,128)(2,1)} %copy.34), calls=%async_computation.2 | async-start | bytes 2097152 | tf_op jit(solution)/shard_map/all_to_all | solution.py:92
  42.5 330.8 %reduce-scatter.3.cloned.1.call-start = ((), (), s32[]{:S(2)}) async-start(), calls=%async_computation.6 | async-start | bytes 14155776 | tf_op jit(solution)/shard_map/reduce_scatter | solution.py:113
  71.2 41.1 %slice-start = ((s8[6291456]{0:T(1024)(128)(4,1)}), s8[2097152]{0:T(1024)(128)(4,1)S(1)}, s32[]{:S(2)}) async-start(s8[6291456]{0:T(1024)(128)(4,1)} %bitcast.146), calls=%async_computation.8 | async-start | bytes 4194304
  76.7 35.6 %slice-start.1 = ((s8[6291456]{0:T(1024)(128)(4,1)}), s8[4194304]{0:T(1024)(128)(4,1)S(1)}, s32[]{:S(2)}) async-start(s8[6291456]{0:T(1024)(128)(4,1)} %bitcast.146), calls=%async_computation.9 | async-start | bytes 8388608
  114.5 40.5 %copy-start.3 = (f32[1,64,8192]{2,1,0:T(8,128)S(1)}, f32[1,64,8192]{2,1,0:T(8,128)}, u32[]{:S(2)}) copy-start(f32[1,64,8192]{2,1,0:T(8,128)} %reshape.130) | copy-start | bytes 6291460
  158.2 35.7 %copy-start.10 = (bf16[1,512,1024]{2,1,0:T(8,128)(2,1)S(1)}, bf16[1,512,1024]{2,1,0:T(8,128)(2,1)}, u32[]{:S(2)}) copy-start(bf16[1,512,1024]{2,1,0:T(8,128)(2,1)} %param.6) | copy-start | bytes 3145732
  160.2 37.0 %copy-start.5 = (bf16[512,1024]{1,0:T(8,128)(2,1)S(1)}, bf16[512,1024]{1,0:T(8,128)(2,1)}, u32[]{:S(2)}) copy-start(bf16[512,1024]{1,0:T(8,128)(2,1)} %get-tuple-element.7) | copy-start | bytes 3145732
  160.2 37.0 %copy-start.6 = (bf16[512,1024]{1,0:T(8,128)(2,1)S(1)}, bf16[512,1024]{1,0:T(8,128)(2,1)}, u32[]{:S(2)}) copy-start(bf16[512,1024]{1,0:T(8,128)(2,1)} %get-tuple-element.8) | copy-start | bytes 3145732
  197.1 5.5 %copy-start.7 = (bf16[512,1024]{1,0:T(8,128)(2,1)}, bf16[512,1024]{1,0:T(8,128)(2,1)S(1)}, u32[]{:S(2)}) copy-start(bf16[512,1024]{1,0:T(8,128)(2,1)S(1)} %get-tuple-element.14) | copy-start | bytes 3145732
  197.4 4.3 collective-permute-start.2
  198.7 3.9 collective-permute-start.3
  215.0 158.3 %copy-start.8 = (bf16[512,1024]{1,0:T(8,128)(2,1)S(1)}, bf16[512,1024]{1,0:T(8,128)(2,1)}, u32[]{:S(2)}) copy-start(bf16[512,1024]{1,0:T(8,128)(2,1)} %copy-done.7) | copy-start | bytes 3145732
  215.0 277.5 %reduce-scatter.5.cloned.1.call-start = ((), (), s32[]{:S(2)}) async-start(), calls=%async_computation.7 | async-start | bytes 1622016 | tf_op jit(solution)/shard_map/reduce_scatter | solution.py:119
  459.0 35.0 %copy-start.1 = (bf16[1,512,1024]{2,1,0:T(8,128)(2,1)S(1)}, bf16[1,512,1024]{2,1,0:T(8,128)(2,1)}, u32[]{:S(2)}) copy-start(bf16[1,512,1024]{2,1,0:T(8,128)(2,1)} %param.5) | copy-start | bytes 3145732
Sparse Core Ops, SparseCore 0:
  215.1 158.0 reduce-scatter.2
  375.9 116.5 reduce-scatter.4
where the time goes:
time: 502 us; the launch traced here: 501 us
  waiting for transfers between devices  206 us (41%)
  blocking collectives  173 us (34%)
  matrix products  43.3 us (9%)
  other arithmetic  25.5 us (5%)
  starting transfers between devices  19.7 us (4%)
  local copies, waits for them, and re-layouts  19.3 us (4%)
  between operations  14.4 us (3%)
    reduce_scatter x1, waiting for transfers between devices, shards(): lax.psum_scatter(lax.dot_general(rows, du, contract, preferred_element_ty...  153 us
    psum x1, blocking collectives, shards(): taps_grad = lax.psum(local_taps, ('dp', 'seq')) * factor  75.7 us
    all_to_all x1, blocking collectives, shards(): lax.all_to_all(block_section(w.reshape(1, nblocks, BLK, width), table_q),...  32.4 us
    all_to_all x1, blocking collectives, shards(): lax.all_to_all(span_section(columns, filt, table_p), 'seq', split_axis=1,...  32.4 us
    all_to_all x1, blocking collectives, shards(): lax.all_to_all(span_section(grad_cols, filt, table_p), 'seq', split_axis=...  32.2 us
    all_to_all x1, waiting for transfers between devices, shards(): lax.all_to_all(block_section(e4.reshape(1, nblocks, BLK, width), table_q)...  26.7 us
    reduce_scatter x1, waiting for transfers between devices, shards(): lax.psum_scatter(partial_sum, 'seq', scatter_dimension=1, tiled=True)  22.5 us
    dot_general x1, matrix products, shards(): lax.dot_general(rows, du, contract, preferred_element_type=jnp.float32)  12.4 us
  transfers between devices with their start and end apart: 7, of which 5 were waited for; matrix products, arithmetic and copies ran while one was open for 6% of the time, Pallas kernels for 0%

commit v1 on v0

--- a/solution.py
+++ b/solution.py
@@ -108,7 +108,7 @@
     dsf = ds.astype(jnp.float32)
     zf = zpad.astype(jnp.float32)
     local_taps = jnp.stack([jnp.sum(dsf * zf[k : k + tok], axis=0) for k in range(3)])
-    taps_grad = lax.psum(local_taps, ("dp", "seq")) * factor
+    taps_grad = lax.psum(lax.psum(local_taps, "seq"), "dp") * factor
     contract = (((0,), (0,)), ((), ()))
     partial_sum = lax.psum_scatter(
         lax.dot_general(rows, du, contract, preferred_element_type=jnp.float32),

time: 502 us -> 549 us (1.094)
  blocking collectives: 173 us -> 242 us
  waiting for transfers between devices: 206 us -> 184 us
    psum x1 -> x2, blocking collectives: 75.7 us -> 145 us  [shards(): taps_grad = lax.psum(lax.psum(local_taps, 'seq'), 'dp') * factor]
    reduce_scatter x1, waiting for transfers between devices: 22.5 us -> 0.01 us  [shards(): lax.psum_scatter(partial_sum, 'seq', scatter_dimension=1, tiled=True)]
  transfers between devices with their start and end apart: 7 -> 7, of which waited for: 5 -> 4; matrix products, arithmetic and copies ran while one was open for 6% -> 5% of each run, Pallas kernels for 0% -> 0%
where the time goes in v1:
time: 549 us; the launch traced here: 548 us
  blocking collectives  242 us (44%)
  waiting for transfers between devices  184 us (34%)
  matrix products  43.2 us (8%)
  other arithmetic  25.5 us (5%)
  starting transfers between devices  19.7 us (4%)
  local copies, waits for them, and re-layouts  19.3 us (4%)
  between operations  14.4 us (3%)
    reduce_scatter x1, waiting for transfers between devices, shards(): lax.psum_scatter(lax.dot_general(rows, du, contract, preferred_element_ty...  153 us
    psum x2, blocking collectives, shards(): taps_grad = lax.psum(lax.psum(local_taps, 'seq'), 'dp') * factor  145 us
    all_to_all x1, blocking collectives, shards(): lax.all_to_all(block_section(w.reshape(1, nblocks, BLK, width), table_q),...  32.5 us
    all_to_all x1, blocking collectives, shards(): lax.all_to_all(span_section(columns, filt, table_p), 'seq', split_axis=1,...  32.4 us
    all_to_all x1, blocking collectives, shards(): lax.all_to_all(span_section(grad_cols, filt, table_p), 'seq', split_axis=...  32.2 us
    all_to_all x1, waiting for transfers between devices, shards(): lax.all_to_all(block_section(e4.reshape(1, nblocks, BLK, width), table_q)...  26.7 us
    dot_general x1, matrix products, shards(): lax.dot_general(rows, du, contract, preferred_element_type=jnp.float32)  12.3 us
    all_to_all x1, starting transfers between devices, shards(): lax.all_to_all(block_section(e4.reshape(1, nblocks, BLK, width), table_q)...  11.8 us
  transfers between devices with their start and end apart: 7, of which 4 were waited for; matrix products, arithmetic and copies ran while one was open for 5% of the time, Pallas kernels for 0%

profile of v1, /device:TPU:2, one launch (start us, length us, event | category | flops | bytes accessed | tf_op | source)
XLA Modules:
  0.0 547.6 jit_solution(397851486052933344)
XLA Ops:
  7.2 1.2 copy-done
  8.4 6.4 %convolution_convert_fusion.2 = bf16[512,3072]{1,0:T(8,128)(2,1)S(1)} fusion(bf16[1024,3072]{1,0:T(8,128)(2,1)} %param.7, bf16[1,512,1024]{2,1,0:T(8,128)(2,1)S(1)} %copy-done), kind=kOutput, calls=%fused_computation.22 | convolution fusion | flops 3222798336 | bytes 10485760 | tf_op jit(solution)/shard_map/dot_general | solution.py:72
  14.9 2.0 collective-permute-start
  16.9 1.3 collective-permute-start.1
  18.2 3.4 collective-permute-done.1
  21.6 2.5 multiply_add_fusion
  24.2 2.7 copy-done.2
  26.8 0.3 fusion.12
  27.2 1.4 fusion.19
  28.6 2.1 copy.34
  30.7 11.8 %all-to-all-start.2 = ((bf16[1,2,256,1024]{3,1,0,2:T(2,128)(2,1)}), bf16[1,2,256,1024]{3,1,0,2:T(2,128)(2,1)S(1)}, u32[]{:S(2)}, u32[]{:S(2)}) async-start(bf16[1,2,256,1024]{3,1,0,2:T(2,128)(2,1)} %copy.34), calls=%async_computation.2 | async-start | bytes 2097152 | tf_op jit(solution)/shard_map/all_to_all | solution.py:92
  42.6 1.6 reshape.130
  44.1 26.7 %all-to-all-done.2 = bf16[1,2,256,1024]{3,1,0,2:T(2,128)(2,1)S(1)} async-done(((bf16[1,2,256,1024]{3,1,0,2:T(2,128)(2,1)}), bf16[1,2,256,1024]{3,1,0,2:T(2,128)(2,1)S(1)}, u32[]{:S(2)}, u32[]{:S(2)}) %all-to-all-start.2) | async-done | bytes 1048608 | tf_op jit(solution)/shard_map/all_to_all | solution.py:92
  70.9 0.3 copy.59
  71.1 0.1 copy.36
  71.2 1.6 copy.47
  72.8 3.8 convolution_convert_fusion
  76.7 2.0 copy.48
  78.6 0.1 bitcast_bitcast_fusion
  78.7 32.2 %all_to_all.60 = bf16[1,64,8,1024]{3,2,0,1:T(8,128)(2,1)S(1)} all-to-all(bf16[1,64,8,1024]{3,2,0,1:T(8,128)(2,1)S(1)} %bitcast_bitcast_fusion), channel_id=1, replica_groups=mesh['dp'=8,'seq'=32] {'seq'}, dimensions={1} | all-to-all | bytes 2097152 | tf_op jit(solution)/shard_map/all_to_all | solution.py:99
  111.0 1.3 fusion.20
  112.3 2.2 fusion.14
  114.6 2.4 fusion.18
  116.9 3.7 copy.27
  120.7 32.5 %all_to_all.61 = bf16[1,2,256,1024]{3,1,0,2:T(2,128)(2,1)S(1)} all-to-all(bf16[1,2,256,1024]{3,1,0,2:T(2,128)(2,1)} %copy.27), channel_id=1, replica_groups=mesh['dp'=8,'seq'=32] {'seq'}, dimensions={2} | all-to-all | bytes 2097152 | tf_op jit(solution)/shard_map/all_to_all | solution.py:81
  153.1 0.3 copy.60
  153.4 0.1 copy.29
  153.5 1.6 copy.45
  155.1 3.2 convolution_convert_fusion.1
  158.2 1.9 copy.46
  160.2 0.1 bitcast_bitcast_fusion.1
  160.3 32.4 %all_to_all.62 = bf16[1,64,8,1024]{3,2,0,1:T(8,128)(2,1)S(1)} all-to-all(bf16[1,64,8,1024]{3,2,0,1:T(8,128)(2,1)S(1)} %bitcast_bitcast_fusion.1), channel_id=1, replica_groups=mesh['dp'=8,'seq'=32] {'seq'}, dimensions={1} | all-to-all | bytes 2097152 | tf_op jit(solution)/shard_map/all_to_all | solution.py:88
  192.6 1.3 fusion.22
  194.0 3.2 fusion.13
  197.2 0.3 pad_maximum_fusion.8
  197.5 1.3 collective-permute-start.2
  198.8 3.0 collective-permute-start.3
  201.9 0.8 collective-permute-done.3
  202.7 12.3 %convolution_bitcast_fusion.2 = f32[1024,3072]{0,1:T(8,128)} fusion(bf16[1,512,1024]{2,1,0:T(8,128)(2,1)S(1)} %copy-done, bf16[1,3072]{1,0:T(2,128)(2,1)S(1)} %collective-permute-done.3, bf16[512,1024]{1,0:T(8,128)(2,1)S(1)} %copy-done.6, bf16[512,1024]{1,0:T(8,128)(2,1)S(1)} %get-tuple-element.14, bf16[512,1024]{1,0:T(8,128)(2,1)S(1)} %copy-done.5, ...), kind=kOutput, calls=%fused_computation.14 | convolution fusion | flops 3265265664 | bytes 16826368 | tf_op jit(solution)/shard_map/dot_general | solution.py:114
  215.0 0.3 reduce-scatter.5.cloned.1.call-start
  215.3 5.5 %maximum_convert_fusion = f32[514,3072]{1,0:T(8,128)} fusion(bf16[1,3072]{1,0:T(2,128)(2,1)S(1)} %collective-permute-done.1, bf16[512,3072]{1,0:T(8,128)(2,1)} %copy-done.4, bf16[1,3072]{1,0:T(2,128)(2,1)S(1)} %collective-permute-done), kind=kLoop, calls=%fused_computation.23 | loop fusion | flops 9474048 | bytes 9474048 | tf_op jit(solution)/shard_map/convert_element_type | solution.py:109
  220.8 152.6 %reduce-scatter.3.cloned.1.call-done = f32[128,3072]{0,1:T(8,128)} async-done(((f32[1024,3072]{0,1:T(8,128)}), f32[128,3072]{0,1:T(8,128)}) %reduce-scatter.3.cloned.1.call-update) | async-done | bytes 1572880 | tf_op jit(solution)/shard_map/reduce_scatter | solution.py:113
  373.4 9.3 %fusion.9 = (f32[3072]{0:T(1024)S(1)}, f32[3072]{0:T(1024)S(1)}, f32[3072]{0:T(1024)S(1)}) fusion(f32[514,3072]{1,0:T(8,128)} %maximum_convert_fusion, bf16[512,1024]{1,0:T(8,128)(2,1)S(1)} %copy-done.6, bf16[512,1024]{1,0:T(8,128)(2,1)S(1)} %copy-done.8, bf16[512,1024]{1,0:T(8,128)(2,1)S(1)} %copy-done.5), kind=kLoop, calls=%fused_computation.18 | loop fusion | flops 18865152 | bytes 22056960 | tf_op jit(solution)/shard_map/reduce_sum | solution.py:110
  382.8 106.6 %psum.14 = f32[3,3072]{1,0:T(4,128)S(1)} all-reduce(f32[3,3072]{1,0:T(4,128)S(1)} %pad_maximum_fusion.9), channel_id=1, replica_groups=mesh['dp'=8,'seq'=32] {'seq'}, use_global_device_ids=true, to_apply=%region_5.6 | all-reduce | flops 9216 | bytes 73728 | tf_op jit(solution)/shard_map/psum | solution.py:111
  489.4 38.3 %psum.15 = f32[3,3072]{1,0:T(4,128)S(1)} all-reduce(f32[3,3072]{1,0:T(4,128)S(1)} %psum.14), channel_id=1, replica_groups=mesh['dp'=8,'seq'=32] {'dp'}, use_global_device_ids=true, to_apply=%region_6.7 | all-reduce | flops 9216 | bytes 73728 | tf_op jit(solution)/shard_map/psum | solution.py:111
  527.6 0.6 broadcast_multiply_fusion
  528.3 11.0 %fusion.17 = bf16[1,512,1024]{2,1,0:T(8,128)(2,1)} fusion(bf16[1024,3072]{1,0:T(8,128)(2,1)} %param.7, bf16[1,3072]{1,0:T(2,128)(2,1)S(1)} %collective-permute-done.3, bf16[512,1024]{1,0:T(8,128)(2,1)S(1)} %copy-done.6, bf16[512,1024]{1,0:T(8,128)(2,1)} %copy-done.7, bf16[512,1024]{1,0:T(8,128)(2,1)S(1)} %copy-done.5, ...), kind=kOutput, calls=%fused_computation.47 | convolution fusion | flops 3265789952 | bytes 10534912 | tf_op jit(solution)/shard_map/dot_general | solution.py:107
  539.3 1.4 broadcast_multiply_fusion.1
  (41 shorter events, 0.3 us)
Async XLA Ops:
  7.2 1.2 copy-start
  7.2 11.0 %copy-start.12 = (f32[3,3072]{1,0:T(4,128)S(1)}, f32[3,3072]{1,0:T(4,128)}, u32[]{:S(2)}) copy-start(f32[3,3072]{1,0:T(4,128)} %param.8) | copy-start | bytes 110596
  14.8 12.4 %copy-start.4 = (bf16[512,3072]{1,0:T(8,128)(2,1)}, bf16[512,3072]{1,0:T(8,128)(2,1)S(1)}, u32[]{:S(2)}) copy-start(bf16[512,3072]{1,0:T(8,128)(2,1)S(1)} %convolution_convert_fusion.2) | copy-start | bytes 9437188
  14.8 12.0 %copy-start.9 = (bf16[1,512,1024]{2,1,0:T(8,128)(2,1)S(1)}, bf16[1,512,1024]{2,1,0:T(8,128)(2,1)}, u32[]{:S(2)}) copy-start(bf16[1,512,1024]{2,1,0:T(8,128)(2,1)} %param.6) | copy-start | bytes 3145732
  14.9 3.4 collective-permute-start
  16.9 4.8 collective-permute-start.1
  24.2 2.7 copy-start.2
  26.8 15.7 %copy-start.11 = (bf16[64,8,1024]{2,1,0:T(8,128)(2,1)S(1)}, bf16[64,8,1024]{2,1,0:T(8,128)(2,1)}, u32[]{:S(2)}) copy-start(bf16[64,8,1024]{2,1,0:T(8,128)(2,1)} %param.9) | copy-start | bytes 3145732
  30.7 40.2 %all-to-all-start.2 = ((bf16[1,2,256,1024]{3,1,0,2:T(2,128)(2,1)}), bf16[1,2,256,1024]{3,1,0,2:T(2,128)(2,1)S(1)}, u32[]{:S(2)}, u32[]{:S(2)}) async-start(bf16[1,2,256,1024]{3,1,0,2:T(2,128)(2,1)} %copy.34), calls=%async_computation.2 | async-start | bytes 2097152 | tf_op jit(solution)/shard_map/all_to_all | solution.py:92
  42.5 330.9 %reduce-scatter.3.cloned.1.call-start = ((), (), s32[]{:S(2)}) async-start(), calls=%async_computation.6 | async-start | bytes 14155776 | tf_op jit(solution)/shard_map/reduce_scatter | solution.py:113
  71.2 41.1 %slice-start = ((s8[6291456]{0:T(1024)(128)(4,1)}), s8[2097152]{0:T(1024)(128)(4,1)S(1)}, s32[]{:S(2)}) async-start(s8[6291456]{0:T(1024)(128)(4,1)} %bitcast.146), calls=%async_computation.8 | async-start | bytes 4194304
  76.7 35.7 %slice-start.1 = ((s8[6291456]{0:T(1024)(128)(4,1)}), s8[4194304]{0:T(1024)(128)(4,1)S(1)}, s32[]{:S(2)}) async-start(s8[6291456]{0:T(1024)(128)(4,1)} %bitcast.146), calls=%async_computation.9 | async-start | bytes 8388608
  114.6 40.5 %copy-start.3 = (f32[1,64,8192]{2,1,0:T(8,128)S(1)}, f32[1,64,8192]{2,1,0:T(8,128)}, u32[]{:S(2)}) copy-start(f32[1,64,8192]{2,1,0:T(8,128)} %reshape.130) | copy-start | bytes 6291460
  158.2 35.7 %copy-start.10 = (bf16[1,512,1024]{2,1,0:T(8,128)(2,1)S(1)}, bf16[1,512,1024]{2,1,0:T(8,128)(2,1)}, u32[]{:S(2)}) copy-start(bf16[1,512,1024]{2,1,0:T(8,128)(2,1)} %param.6) | copy-start | bytes 3145732
  160.2 37.0 %copy-start.5 = (bf16[512,1024]{1,0:T(8,128)(2,1)S(1)}, bf16[512,1024]{1,0:T(8,128)(2,1)}, u32[]{:S(2)}) copy-start(bf16[512,1024]{1,0:T(8,128)(2,1)} %get-tuple-element.7) | copy-start | bytes 3145732
  160.2 37.0 %copy-start.6 = (bf16[512,1024]{1,0:T(8,128)(2,1)S(1)}, bf16[512,1024]{1,0:T(8,128)(2,1)}, u32[]{:S(2)}) copy-start(bf16[512,1024]{1,0:T(8,128)(2,1)} %get-tuple-element.8) | copy-start | bytes 3145732
  197.2 5.5 copy-start.7
  197.5 4.3 collective-permute-start.2
  198.8 3.9 collective-permute-start.3
  215.0 158.3 %copy-start.8 = (bf16[512,1024]{1,0:T(8,128)(2,1)S(1)}, bf16[512,1024]{1,0:T(8,128)(2,1)}, u32[]{:S(2)}) copy-start(bf16[512,1024]{1,0:T(8,128)(2,1)} %copy-done.7) | copy-start | bytes 3145732
  215.0 324.2 %reduce-scatter.5.cloned.1.call-start = ((), (), s32[]{:S(2)}) async-start(), calls=%async_computation.7 | async-start | bytes 1622016 | tf_op jit(solution)/shard_map/reduce_scatter | solution.py:119
  528.3 12.4 %copy-start.1 = (bf16[1,512,1024]{2,1,0:T(8,128)(2,1)S(1)}, bf16[1,512,1024]{2,1,0:T(8,128)(2,1)}, u32[]{:S(2)}) copy-start(bf16[1,512,1024]{2,1,0:T(8,128)(2,1)} %param.5) | copy-start | bytes 3145732
Sparse Core Ops, SparseCore 0:
  215.2 158.1 reduce-scatter.2
  376.0 116.8 reduce-scatter.4
